TPU v7x, 128 devices: a whole 4x4x4 slice. The times are simulated.
128 devices in a mesh: blk: 8 (over z_lo, y), inner: 16 (over x, z_hi, core).
Axes of the slice: x: 4, y: 4, z: 4 (z_hi: 2, z_lo: 2; z = z_hi * 2 + z_lo), core: 2. Of those that a mesh axis runs over, the one named last changes fastest.
Arguments:
- queries: bfloat16 [16384, 768], P(('blk', 'inner')), may hold values from -16 to 16
- keys: bfloat16 [16384, 768], P(('blk', 'inner')), may hold values from -16 to 16
- values: bfloat16 [16384, 768], P(('blk', 'inner')), may hold values from -6 to 6
- valid: int32 [16384], P(('blk', 'inner')), may hold values 0 or 1
- out_weight: bfloat16 [768, 768], replicated, may hold values from -0.21875 to 0.21875
Outputs:
- mixed: bfloat16 [16384, 768], P(('blk', 'inner'))
All inputs are finite; a program needn't handle non-finite values. No bound on the sum of `valid` on one device may be relied on, other than what follows from the above.
Results may differ from a plain program's by a relative error of at most 0.015.
Values may be sent and summed in bfloat16 or wider, within the bound.
A program may use at most 128 MiB of HBM per device.

v0:
```python
import jax
import jax.numpy as jnp
from jax import lax
from jax.sharding import PartitionSpec as P

HEADS = 12
HEAD_DIM = 64


def make_fold(query_all):
    query_count = query_all.shape[0]
    query_heads = query_all.reshape(query_count, HEADS, HEAD_DIM)
    score_scale = HEAD_DIM ** (-0.5)

    def attend(state_now, piece, start):
        key_piece, value_piece, flag_piece = piece
        piece_rows = key_piece.shape[0]
        block_rows = 128
        count = piece_rows // block_rows
        key_blocks = key_piece.reshape(count, block_rows, HEADS, HEAD_DIM)
        value_blocks = value_piece.reshape(count, block_rows, HEADS, HEAD_DIM)
        flag_blocks = flag_piece.reshape(count, block_rows)

        def one_block(carry, item):
            run_max, row_total, weighted = carry
            key_heads, value_heads, flag_block = item
            scores = (
                jnp.einsum(
                    "qhd,khd->hqk", query_heads, key_heads, preferred_element_type=jnp.float32
                )
                * score_scale
            )
            scores = jnp.where(flag_block[None, None, :] > 0, scores, -1e30)
            new_max = jnp.maximum(run_max, jnp.max(scores, axis=-1))
            shrink = jnp.exp(run_max - new_max)
            chances = jnp.exp(scores - new_max[..., None]).astype(jnp.bfloat16)
            row_total = row_total * shrink + jnp.sum(chances, axis=-1, dtype=jnp.float32)
            weighted = weighted * shrink[..., None] + jnp.einsum(
                "hqk,khd->hqd", chances, value_heads, preferred_element_type=jnp.float32
            )
            return ((new_max, row_total, weighted), None)

        state_end, unused = lax.scan(one_block, state_now, (key_blocks, value_blocks, flag_blocks))
        return state_end

    starting = (
        jnp.zeros((HEADS, query_count), jnp.float32),
        jnp.zeros((HEADS, query_count), jnp.float32),
        jnp.zeros((HEADS, query_count, HEAD_DIM), jnp.float32),
    )
    return (attend, starting)


def settle(top, row_total, weighted):
    return weighted / (jnp.exp(-top) + row_total)[..., None]


def combine_loop(state_end, own_rows):
    run_max, row_total, weighted = state_end
    top = lax.pmax(run_max, "blk")
    shrink = jnp.exp(run_max - top)
    total_own, weighted_own = (
        lax.psum_scatter(row_total * shrink, "blk", scatter_dimension=1, tiled=True),
        lax.psum_scatter(weighted * shrink[..., None], "blk", scatter_dimension=1, tiled=True),
    )
    top_own = lax.dynamic_slice_in_dim(top, lax.axis_index("blk") * own_rows, own_rows, 1)
    return settle(top_own, total_own, weighted_own)


def on_device(queries, keys, values, valid, out_weight):
    own_rows = queries.shape[0]
    width = queries.shape[1]
    flags = valid.astype(jnp.bfloat16)
    query_all = lax.all_gather(queries, "blk", axis=0, tiled=True)
    attend, starting = make_fold(query_all)
    state_end = attend(
        starting,
        (
            lax.all_gather(keys, "inner", axis=0, tiled=True),
            lax.all_gather(values, "inner", axis=0, tiled=True),
            lax.all_gather(flags, "inner", axis=0, tiled=True),
        ),
        jnp.int32(0),
    )
    attended = combine_loop(state_end, own_rows)
    attended = jnp.transpose(attended, (1, 0, 2)).reshape(own_rows, width).astype(jnp.bfloat16)
    return jnp.dot(attended, out_weight, preferred_element_type=jnp.float32).astype(jnp.bfloat16)


def solution(mesh):
    return jax.shard_map(
        on_device,
        mesh=mesh,
        in_specs=(
            P(("blk", "inner"), None),
            P(("blk", "inner"), None),
            P(("blk", "inner"), None),
            P(("blk", "inner")),
            P(),
        ),
        out_specs=P(("blk", "inner"), None),
        check_vma=False,
    )
```

profile of v0, /device:TPU:0, one launch (start us, length us, event | category | flops | bytes accessed | tf_op | source)
XLA Modules:
  0.0 532.3 jit_solution(9887534371943158650)
XLA Ops:
  9.5 25.0 %all-gather = bf16[16,1,128]{2,1,0:T(2,128)(2,1)S(1)} all-gather(bf16[1,1,128]{2,1,0:T(2,128)(2,1)S(1)} %convert_bitcast_fusion), channel_id=1, replica_groups=mesh['blk'=8,'inner'=16] {'inner'}, dimensions={0}, use_global_device_ids=true | all-gather | bytes 4352 | tf_op jit(solution)/shard_map/all_gather | solution.py:81
  34.4 17.7 %all-gather.7.cloned.1.call-done = bf16[1024,768]{1,0:T(8,128)(2,1)} async-done(((bf16[128,768]{1,0:T(8,128)(2,1)}), bf16[1024,768]{1,0:T(8,128)(2,1)}) %all-gather.7.cloned.1.call-update) | async-done | bytes 1572880 | tf_op jit(solution)/shard_map/all_gather | solution.py:74
  53.8 52.2 %all-gather.5.cloned.1.call-done = bf16[2048,768]{1,0:T(8,128)(2,1)} async-done(((bf16[128,768]{1,0:T(8,128)(2,1)}), bf16[2048,768]{1,0:T(8,128)(2,1)}) %all-gather.5.cloned.1.call-update) | async-done | bytes 3145744 | tf_op jit(solution)/shard_map/all_gather | solution.py:79
  116.3 43.1 %all-gather.9.cloned.1.call-done = bf16[2048,768]{1,0:T(8,128)(2,1)} async-done(((bf16[128,768]{1,0:T(8,128)(2,1)}), bf16[2048,768]{1,0:T(8,128)(2,1)}) %all-gather.9.cloned.1.call-update) | async-done | bytes 3145744 | tf_op jit(solution)/shard_map/all_gather | solution.py:80
  169.5 238.6 %while.15 = (s32[]{:T(128)}, f32[12,1024]{1,0:T(8,128)S(1)}, f32[12,1024]{1,0:T(8,128)S(1)}, f32[12,1024,64]{1,2,0:T(8,128)}, bf16[16,128]{1,0:T(8,128)(2,1)S(1)...) while((s32[]{:T(128)}, f32[12,1024]{1,0:T(8,128)S(1)}, ...), condition=%wide.region_3.4_spmd.clone, body=%wide.region_0.3_spmd.clone.sunk | while | flops 425521536 | bytes 53086096 | solution.py:43
  169.5 4.8 bitcast_reduce_fusion.2
  192.8 5.5 %fusion.25 = f32[12,1024,64]{1,2,0:T(8,128)} fusion(f32[12,1024,64]{1,2,0:T(8,128)} %get-tuple-element.187, f32[12,1024]{1,0:T(8,128)S(1)} %get-tuple-element.173, pred[]{:T(512)S(6)} %compare.3, bf16[16,128,12,64]{1,3,2,0:T(8,128)(2,1)} %get-tuple-element.201, s32[]{:T(128)} %get-tuple-element.184, f32[12,128,1024]{2,1,0:T(8,128)S(1)} %copy-done.1, ...), kind=kOutput, calls=%fused_computation.7.clone.1 | convolution fusion | flops 209977344 | bytes 12878465 | tf_op jit(solution)/shard_map/while/body/eval_jaxpr/hqk,khd->hqd/dot_general | solution.py:38
  207.8 5.5 %fusion.25 = f32[12,1024,64]{1,2,0:T(8,128)} fusion(f32[12,1024,64]{1,2,0:T(8,128)} %get-tuple-element.187, f32[12,1024]{1,0:T(8,128)S(1)} %get-tuple-element.173, pred[]{:T(512)S(6)} %compare.3, bf16[16,128,12,64]{1,3,2,0:T(8,128)(2,1)} %get-tuple-element.201, s32[]{:T(128)} %get-tuple-element.184, f32[12,128,1024]{2,1,0:T(8,128)S(1)} %copy-done.1, ...), kind=kOutput, calls=%fused_computation.7.clone.1 | convolution fusion | flops 209977344 | bytes 12878465 | tf_op jit(solution)/shard_map/while/body/eval_jaxpr/hqk,khd->hqd/dot_general | solution.py:38
  222.8 5.5 %fusion.25 = f32[12,1024,64]{1,2,0:T(8,128)} fusion(f32[12,1024,64]{1,2,0:T(8,128)} %get-tuple-element.187, f32[12,1024]{1,0:T(8,128)S(1)} %get-tuple-element.173, pred[]{:T(512)S(6)} %compare.3, bf16[16,128,12,64]{1,3,2,0:T(8,128)(2,1)} %get-tuple-element.201, s32[]{:T(128)} %get-tuple-element.184, f32[12,128,1024]{2,1,0:T(8,128)S(1)} %copy-done.1, ...), kind=kOutput, calls=%fused_computation.7.clone.1 | convolution fusion | flops 209977344 | bytes 12878465 | tf_op jit(solution)/shard_map/while/body/eval_jaxpr/hqk,khd->hqd/dot_general | solution.py:38
  237.8 5.5 %fusion.25 = f32[12,1024,64]{1,2,0:T(8,128)} fusion(f32[12,1024,64]{1,2,0:T(8,128)} %get-tuple-element.187, f32[12,1024]{1,0:T(8,128)S(1)} %get-tuple-element.173, pred[]{:T(512)S(6)} %compare.3, bf16[16,128,12,64]{1,3,2,0:T(8,128)(2,1)} %get-tuple-element.201, s32[]{:T(128)} %get-tuple-element.184, f32[12,128,1024]{2,1,0:T(8,128)S(1)} %copy-done.1, ...), kind=kOutput, calls=%fused_computation.7.clone.1 | convolution fusion | flops 209977344 | bytes 12878465 | tf_op jit(solution)/shard_map/while/body/eval_jaxpr/hqk,khd->hqd/dot_general | solution.py:38
  252.7 5.5 %fusion.25 = f32[12,1024,64]{1,2,0:T(8,128)} fusion(f32[12,1024,64]{1,2,0:T(8,128)} %get-tuple-element.187, f32[12,1024]{1,0:T(8,128)S(1)} %get-tuple-element.173, pred[]{:T(512)S(6)} %compare.3, bf16[16,128,12,64]{1,3,2,0:T(8,128)(2,1)} %get-tuple-element.201, s32[]{:T(128)} %get-tuple-element.184, f32[12,128,1024]{2,1,0:T(8,128)S(1)} %copy-done.1, ...), kind=kOutput, calls=%fused_computation.7.clone.1 | convolution fusion | flops 209977344 | bytes 12878465 | tf_op jit(solution)/shard_map/while/body/eval_jaxpr/hqk,khd->hqd/dot_general | solution.py:38
  267.7 5.5 %fusion.25 = f32[12,1024,64]{1,2,0:T(8,128)} fusion(f32[12,1024,64]{1,2,0:T(8,128)} %get-tuple-element.187, f32[12,1024]{1,0:T(8,128)S(1)} %get-tuple-element.173, pred[]{:T(512)S(6)} %compare.3, bf16[16,128,12,64]{1,3,2,0:T(8,128)(2,1)} %get-tuple-element.201, s32[]{:T(128)} %get-tuple-element.184, f32[12,128,1024]{2,1,0:T(8,128)S(1)} %copy-done.1, ...), kind=kOutput, calls=%fused_computation.7.clone.1 | convolution fusion | flops 209977344 | bytes 12878465 | tf_op jit(solution)/shard_map/while/body/eval_jaxpr/hqk,khd->hqd/dot_general | solution.py:38
  282.7 5.5 %fusion.25 = f32[12,1024,64]{1,2,0:T(8,128)} fusion(f32[12,1024,64]{1,2,0:T(8,128)} %get-tuple-element.187, f32[12,1024]{1,0:T(8,128)S(1)} %get-tuple-element.173, pred[]{:T(512)S(6)} %compare.3, bf16[16,128,12,64]{1,3,2,0:T(8,128)(2,1)} %get-tuple-element.201, s32[]{:T(128)} %get-tuple-element.184, f32[12,128,1024]{2,1,0:T(8,128)S(1)} %copy-done.1, ...), kind=kOutput, calls=%fused_computation.7.clone.1 | convolution fusion | flops 209977344 | bytes 12878465 | tf_op jit(solution)/shard_map/while/body/eval_jaxpr/hqk,khd->hqd/dot_general | solution.py:38
  297.7 5.5 %fusion.25 = f32[12,1024,64]{1,2,0:T(8,128)} fusion(f32[12,1024,64]{1,2,0:T(8,128)} %get-tuple-element.187, f32[12,1024]{1,0:T(8,128)S(1)} %get-tuple-element.173, pred[]{:T(512)S(6)} %compare.3, bf16[16,128,12,64]{1,3,2,0:T(8,128)(2,1)} %get-tuple-element.201, s32[]{:T(128)} %get-tuple-element.184, f32[12,128,1024]{2,1,0:T(8,128)S(1)} %copy-done.1, ...), kind=kOutput, calls=%fused_computation.7.clone.1 | convolution fusion | flops 209977344 | bytes 12878465 | tf_op jit(solution)/shard_map/while/body/eval_jaxpr/hqk,khd->hqd/dot_general | solution.py:38
  312.7 5.5 %fusion.25 = f32[12,1024,64]{1,2,0:T(8,128)} fusion(f32[12,1024,64]{1,2,0:T(8,128)} %get-tuple-element.187, f32[12,1024]{1,0:T(8,128)S(1)} %get-tuple-element.173, pred[]{:T(512)S(6)} %compare.3, bf16[16,128,12,64]{1,3,2,0:T(8,128)(2,1)} %get-tuple-element.201, s32[]{:T(128)} %get-tuple-element.184, f32[12,128,1024]{2,1,0:T(8,128)S(1)} %copy-done.1, ...), kind=kOutput, calls=%fused_computation.7.clone.1 | convolution fusion | flops 209977344 | bytes 12878465 | tf_op jit(solution)/shard_map/while/body/eval_jaxpr/hqk,khd->hqd/dot_general | solution.py:38
  327.6 5.5 %fusion.25 = f32[12,1024,64]{1,2,0:T(8,128)} fusion(f32[12,1024,64]{1,2,0:T(8,128)} %get-tuple-element.187, f32[12,1024]{1,0:T(8,128)S(1)} %get-tuple-element.173, pred[]{:T(512)S(6)} %compare.3, bf16[16,128,12,64]{1,3,2,0:T(8,128)(2,1)} %get-tuple-element.201, s32[]{:T(128)} %get-tuple-element.184, f32[12,128,1024]{2,1,0:T(8,128)S(1)} %copy-done.1, ...), kind=kOutput, calls=%fused_computation.7.clone.1 | convolution fusion | flops 209977344 | bytes 12878465 | tf_op jit(solution)/shard_map/while/body/eval_jaxpr/hqk,khd->hqd/dot_general | solution.py:38
  342.6 5.5 %fusion.25 = f32[12,1024,64]{1,2,0:T(8,128)} fusion(f32[12,1024,64]{1,2,0:T(8,128)} %get-tuple-element.187, f32[12,1024]{1,0:T(8,128)S(1)} %get-tuple-element.173, pred[]{:T(512)S(6)} %compare.3, bf16[16,128,12,64]{1,3,2,0:T(8,128)(2,1)} %get-tuple-element.201, s32[]{:T(128)} %get-tuple-element.184, f32[12,128,1024]{2,1,0:T(8,128)S(1)} %copy-done.1, ...), kind=kOutput, calls=%fused_computation.7.clone.1 | convolution fusion | flops 209977344 | bytes 12878465 | tf_op jit(solution)/shard_map/while/body/eval_jaxpr/hqk,khd->hqd/dot_general | solution.py:38
  357.6 5.5 %fusion.25 = f32[12,1024,64]{1,2,0:T(8,128)} fusion(f32[12,1024,64]{1,2,0:T(8,128)} %get-tuple-element.187, f32[12,1024]{1,0:T(8,128)S(1)} %get-tuple-element.173, pred[]{:T(512)S(6)} %compare.3, bf16[16,128,12,64]{1,3,2,0:T(8,128)(2,1)} %get-tuple-element.201, s32[]{:T(128)} %get-tuple-element.184, f32[12,128,1024]{2,1,0:T(8,128)S(1)} %copy-done.1, ...), kind=kOutput, calls=%fused_computation.7.clone.1 | convolution fusion | flops 209977344 | bytes 12878465 | tf_op jit(solution)/shard_map/while/body/eval_jaxpr/hqk,khd->hqd/dot_general | solution.py:38
  372.6 5.5 %fusion.25 = f32[12,1024,64]{1,2,0:T(8,128)} fusion(f32[12,1024,64]{1,2,0:T(8,128)} %get-tuple-element.187, f32[12,1024]{1,0:T(8,128)S(1)} %get-tuple-element.173, pred[]{:T(512)S(6)} %compare.3, bf16[16,128,12,64]{1,3,2,0:T(8,128)(2,1)} %get-tuple-element.201, s32[]{:T(128)} %get-tuple-element.184, f32[12,128,1024]{2,1,0:T(8,128)S(1)} %copy-done.1, ...), kind=kOutput, calls=%fused_computation.7.clone.1 | convolution fusion | flops 209977344 | bytes 12878465 | tf_op jit(solution)/shard_map/while/body/eval_jaxpr/hqk,khd->hqd/dot_general | solution.py:38
  387.6 5.5 %fusion.25 = f32[12,1024,64]{1,2,0:T(8,128)} fusion(f32[12,1024,64]{1,2,0:T(8,128)} %get-tuple-element.187, f32[12,1024]{1,0:T(8,128)S(1)} %get-tuple-element.173, pred[]{:T(512)S(6)} %compare.3, bf16[16,128,12,64]{1,3,2,0:T(8,128)(2,1)} %get-tuple-element.201, s32[]{:T(128)} %get-tuple-element.184, f32[12,128,1024]{2,1,0:T(8,128)S(1)} %copy-done.1, ...), kind=kOutput, calls=%fused_computation.7.clone.1 | convolution fusion | flops 209977344 | bytes 12878465 | tf_op jit(solution)/shard_map/while/body/eval_jaxpr/hqk,khd->hqd/dot_general | solution.py:38
  402.6 5.5 %fusion.25 = f32[12,1024,64]{1,2,0:T(8,128)} fusion(f32[12,1024,64]{1,2,0:T(8,128)} %get-tuple-element.187, f32[12,1024]{1,0:T(8,128)S(1)} %get-tuple-element.173, pred[]{:T(512)S(6)} %compare.3, bf16[16,128,12,64]{1,3,2,0:T(8,128)(2,1)} %get-tuple-element.201, s32[]{:T(128)} %get-tuple-element.184, f32[12,128,1024]{2,1,0:T(8,128)S(1)} %copy-done.1, ...), kind=kOutput, calls=%fused_computation.7.clone.1 | convolution fusion | flops 209977344 | bytes 12878465 | tf_op jit(solution)/shard_map/while/body/eval_jaxpr/hqk,khd->hqd/dot_general | solution.py:38
  408.1 33.8 %pmax.7 = f32[12,1024]{1,0:T(8,128)S(1)} all-reduce(f32[12,1024]{1,0:T(8,128)S(1)} %get-tuple-element.50), channel_id=1, replica_groups=mesh['blk'=8,'inner'=16] {'blk'}, use_global_device_ids=true, to_apply=%region_4.5 | all-reduce | flops 12288 | bytes 98304 | tf_op jit(solution)/shard_map/pmax | solution.py:60
  446.8 29.9 %reduce-scatter.5.cloned.1.call-done = f32[12,128]{1,0:T(8,128)} async-done(((f32[12,1024]{1,0:T(8,128)}), f32[12,128]{1,0:T(8,128)}) %reduce-scatter.5.cloned.1.call-update) | async-done | bytes 6160 | tf_op jit(solution)/shard_map/reduce_scatter | solution.py:63
  477.3 46.4 %reduce-scatter.3.cloned.1.call-done = f32[12,128,64]{1,2,0:T(8,128)} async-done(((f32[12,1024,64]{1,2,0:T(8,128)}), f32[12,128,64]{1,2,0:T(8,128)}) %reduce-scatter.3.cloned.1.call-update) | async-done | bytes 393232 | tf_op jit(solution)/shard_map/reduce_scatter | solution.py:64
  (157 shorter events, 183.0 us)
Async XLA Ops:
  6.5 518.2 %copy-start = (bf16[768,768]{1,0:T(8,128)(2,1)S(1)}, bf16[768,768]{1,0:T(8,128)(2,1)}, u32[]{:S(2)}) copy-start(bf16[768,768]{1,0:T(8,128)(2,1)} %param.11) | copy-start | bytes 3538948
  6.5 45.6 %all-gather.7.cloned.1.call-start = ((), (), s32[]{:S(2)}) async-start(), calls=%async_computation.3 | async-start | bytes 1769472 | tf_op jit(solution)/shard_map/all_gather | solution.py:74
  7.3 98.8 %all-gather.5.cloned.1.call-start = ((), (), s32[]{:S(2)}) async-start(), calls=%async_computation.2 | async-start | bytes 3342336 | tf_op jit(solution)/shard_map/all_gather | solution.py:79
  8.0 151.4 %all-gather.9.cloned.1.call-start = ((), (), s32[]{:S(2)}) async-start(), calls=%async_computation.4 | async-start | bytes 3342336 | tf_op jit(solution)/shard_map/all_gather | solution.py:80
  8.7 467.9 %reduce-scatter.5.cloned.1.call-start = ((), (), s32[]{:S(2)}) async-start(), calls=%async_computation.6 | async-start | bytes 73728 | tf_op jit(solution)/shard_map/reduce_scatter | solution.py:63
  174.3 4.6 copy-start.1
  188.2 4.6 copy-start.1
  203.2 4.6 copy-start.1
  218.2 4.6 copy-start.1
  233.2 4.6 copy-start.1
  248.1 4.6 copy-start.1
  263.1 4.6 copy-start.1
  278.1 4.6 copy-start.1
  293.1 4.6 copy-start.1
  308.1 4.6 copy-start.1
  323.0 4.6 copy-start.1
  338.0 4.6 copy-start.1
  353.0 4.6 copy-start.1
  368.0 4.6 copy-start.1
  383.0 4.6 copy-start.1
  398.0 4.6 copy-start.1
  442.5 81.2 %reduce-scatter.3.cloned.1.call-start = ((), (), s32[]{:S(2)}) async-start(), calls=%async_computation.5 | async-start | bytes 3538944 | tf_op jit(solution)/shard_map/reduce_scatter | solution.py:64
Sparse Core Ops, SparseCore 0:
  9.0 43.0 all-gather.6
  54.5 51.5 all-gather.4
  108.5 50.8 all-gather.8
  442.6 33.9 reduce-scatter.4
  479.0 44.6 reduce-scatter.2
where the time goes:
time: 534 us; the launch traced here: 532 us
  waiting for transfers between devices  191 us (36%)
  matrix products  166 us (31%)
  other arithmetic  77.2 us (14%)
  blocking collectives  58.7 us (11%)
  local copies, waits for them, and re-layouts  25.7 us (5%)
  between operations  13.2 us (2%)
    dot_general x16, matrix products, one_block(): jnp.einsum('hqk,khd->hqd', chances, value_heads, preferred_element_type=j...  87.4 us
    dot_general x16, matrix products, one_block(): jnp.einsum('qhd,khd->hqk', query_heads, key_heads, preferred_element_type...  77.1 us
    reduce_sum x16, other arithmetic, one_block(): jnp.sum(chances, axis=-1, dtype=jnp.float32)  69 us
    all_gather x1, waiting for transfers between devices, on_device(): lax.all_gather(keys, 'inner', axis=0, tiled=True)  52.2 us
    reduce_scatter x1, waiting for transfers between devices, combine_loop(): lax.psum_scatter(weighted * shrink[..., None], 'blk', scatter_dimension=1...  46.4 us
    all_gather x1, waiting for transfers between devices, on_device(): lax.all_gather(values, 'inner', axis=0, tiled=True)  43.1 us
    pmax x1, blocking collectives, combine_loop(): top = lax.pmax(run_max, 'blk')  33.8 us
    reduce_scatter x1, waiting for transfers between devices, combine_loop(): lax.psum_scatter(row_total * shrink, 'blk', scatter_dimension=1, tiled=True)  29.9 us
  transfers between devices with their start and end apart: 5, of which 5 were waited for; matrix products, arithmetic and copies ran while one was open for 3% of the time, Pallas kernels for 0%

commit v1 on v0

--- a/solution.py
+++ b/solution.py
@@ -76,7 +76,9 @@
     state_end = attend(
         starting,
         (
-            lax.all_gather(keys, "inner", axis=0, tiled=True),
+            jnp.concatenate(
+                jax.lax.all_to_all(jnp.stack([keys] * jax.lax.axis_size("inner")), "inner", 0, 0), 0
+            ),
             lax.all_gather(values, "inner", axis=0, tiled=True),
             lax.all_gather(flags, "inner", axis=0, tiled=True),
         ),

time: 534 us -> 490 us (0.918)
  waiting for transfers between devices: 191 us -> 105 us
  blocking collectives: 58.7 us -> 101 us
  starting transfers between devices: 0.16 us -> 8.1 us
  local copies, waits for them, and re-layouts: 25.7 us -> 18.9 us
    all_gather x1 -> x0, waiting for transfers between devices: 52.2 us -> none  [on_device(): lax.all_gather(keys, 'inner', axis=0, tiled=True)]
    all_gather x1, blocking collectives: 25 us -> 67.4 us  [on_device(): lax.all_gather(flags, 'inner', axis=0, tiled=True)]
    all_gather x1, waiting for transfers between devices: 17.7 us -> 0.01 us  [on_device(): query_all = lax.all_gather(queries, 'blk', axis=0, tiled=True)]
    all_gather x1, waiting for transfers between devices: 43.1 us -> 27.5 us  [on_device(): lax.all_gather(values, 'inner', axis=0, tiled=True)]
    all_to_all x0 -> x1, starting transfers between devices: none -> 7.98 us  [on_device(): jax.lax.all_to_all(jnp.stack([keys] * jax.lax.axis_size('inner')), 'inner...]
    unnamed x7 -> x8, local copies, waits for them, and re-layouts: 10.9 us -> 6.5 us
  transfers between devices with their start and end apart: 5 -> 5, of which waited for: 5 -> 3; matrix products, arithmetic and copies ran while one was open for 3% -> 4% of each run, Pallas kernels for 0% -> 0%
where the time goes in v1:
time: 490 us; the launch traced here: 489 us
  matrix products  166 us (34%)
  waiting for transfers between devices  105 us (21%)
  blocking collectives  101 us (21%)
  other arithmetic  76.5 us (16%)
  local copies, waits for them, and re-layouts  18.9 us (4%)
  between operations  13.2 us (3%)
  starting transfers between devices  8.1 us (2%)
    dot_general x16, matrix products, one_block(): jnp.einsum('hqk,khd->hqd', chances, value_heads, preferred_element_type=j...  87.4 us
    dot_general x16, matrix products, one_block(): jnp.einsum('qhd,khd->hqk', query_heads, key_heads, preferred_element_type...  77.1 us
    reduce_sum x16, other arithmetic, one_block(): jnp.sum(chances, axis=-1, dtype=jnp.float32)  69 us
    all_gather x1, blocking collectives, on_device(): lax.all_gather(flags, 'inner', axis=0, tiled=True)  67.4 us
    reduce_scatter x1, waiting for transfers between devices, combine_loop(): lax.psum_scatter(weighted * shrink[..., None], 'blk', scatter_dimension=1...  46.5 us
    pmax x1, blocking collectives, combine_loop(): top = lax.pmax(run_max, 'blk')  33.8 us
    reduce_scatter x1, waiting for transfers between devices, combine_loop(): lax.psum_scatter(row_total * shrink, 'blk', scatter_dimension=1, tiled=True)  29.9 us
    all_gather x1, waiting for transfers between devices, on_device(): lax.all_gather(values, 'inner', axis=0, tiled=True)  27.5 us
  transfers between devices with their start and end apart: 5, of which 3 were waited for; matrix products, arithmetic and copies ran while one was open for 4% of the time, Pallas kernels for 0%

profile of v1, /device:TPU:0, one launch (start us, length us, event | category | flops | bytes accessed | tf_op | source)
XLA Modules:
  0.0 489.2 jit_solution(9422314213067358289)
XLA Ops:
  11.4 8.0 %all-to-all-start = ((bf16[16,128,768]{1,2,0:T(8,128)(2,1)}), bf16[16,128,768]{1,2,0:T(8,128)(2,1)}, u32[]{:S(2)}, u32[]{:S(2)}) async-start(bf16[16,128,768]{1,2,0:T(8,128)(2,1)} %stack.2), calls=%async_computation | async-start | bytes 6291456 | tf_op jit(solution)/shard_map/all_to_all | solution.py:80
  19.4 67.4 %all-gather = bf16[16,1,128]{2,1,0:T(2,128)(2,1)S(1)} all-gather(bf16[1,1,128]{2,1,0:T(2,128)(2,1)S(1)} %convert_bitcast_fusion), channel_id=1, replica_groups=mesh['blk'=8,'inner'=16] {'inner'}, dimensions={0}, use_global_device_ids=true | all-gather | bytes 4352 | tf_op jit(solution)/shard_map/all_gather | solution.py:83
  88.6 27.5 %all-gather.6.cloned.1.call-done = bf16[2048,768]{1,0:T(8,128)(2,1)} async-done(((bf16[128,768]{1,0:T(8,128)(2,1)}), bf16[2048,768]{1,0:T(8,128)(2,1)}) %all-gather.6.cloned.1.call-update) | async-done | bytes 3145744 | tf_op jit(solution)/shard_map/all_gather | solution.py:82
  126.2 238.6 %while.15 = (s32[]{:T(128)}, f32[12,1024]{1,0:T(8,128)S(1)}, f32[12,1024]{1,0:T(8,128)S(1)}, f32[12,1024,64]{1,2,0:T(8,128)}, bf16[16,128]{1,0:T(8,128)(2,1)S(1)...) while((s32[]{:T(128)}, f32[12,1024]{1,0:T(8,128)S(1)}, ...), condition=%wide.region_3.4_spmd.clone, body=%wide.region_0.3_spmd.clone.sunk | while | flops 425521536 | bytes 53086096 | solution.py:43
  140.2 4.8 bitcast_reduce_fusion.2
  149.6 5.5 %fusion.25 = f32[12,1024,64]{1,2,0:T(8,128)} fusion(f32[12,1024,64]{1,2,0:T(8,128)} %get-tuple-element.187, f32[12,1024]{1,0:T(8,128)S(1)} %get-tuple-element.173, pred[]{:T(512)S(6)} %compare.3, bf16[16,128,12,64]{1,3,2,0:T(8,128)(2,1)} %get-tuple-element.201, s32[]{:T(128)} %get-tuple-element.184, f32[12,128,1024]{2,1,0:T(8,128)S(1)} %copy-done.1, ...), kind=kOutput, calls=%fused_computation.7.clone.1 | convolution fusion | flops 209977344 | bytes 12878465 | tf_op jit(solution)/shard_map/while/body/eval_jaxpr/hqk,khd->hqd/dot_general | solution.py:38
  155.1 4.8 bitcast_reduce_fusion.2
  164.6 5.5 %fusion.25 = f32[12,1024,64]{1,2,0:T(8,128)} fusion(f32[12,1024,64]{1,2,0:T(8,128)} %get-tuple-element.187, f32[12,1024]{1,0:T(8,128)S(1)} %get-tuple-element.173, pred[]{:T(512)S(6)} %compare.3, bf16[16,128,12,64]{1,3,2,0:T(8,128)(2,1)} %get-tuple-element.201, s32[]{:T(128)} %get-tuple-element.184, f32[12,128,1024]{2,1,0:T(8,128)S(1)} %copy-done.1, ...), kind=kOutput, calls=%fused_computation.7.clone.1 | convolution fusion | flops 209977344 | bytes 12878465 | tf_op jit(solution)/shard_map/while/body/eval_jaxpr/hqk,khd->hqd/dot_general | solution.py:38
  179.6 5.5 %fusion.25 = f32[12,1024,64]{1,2,0:T(8,128)} fusion(f32[12,1024,64]{1,2,0:T(8,128)} %get-tuple-element.187, f32[12,1024]{1,0:T(8,128)S(1)} %get-tuple-element.173, pred[]{:T(512)S(6)} %compare.3, bf16[16,128,12,64]{1,3,2,0:T(8,128)(2,1)} %get-tuple-element.201, s32[]{:T(128)} %get-tuple-element.184, f32[12,128,1024]{2,1,0:T(8,128)S(1)} %copy-done.1, ...), kind=kOutput, calls=%fused_computation.7.clone.1 | convolution fusion | flops 209977344 | bytes 12878465 | tf_op jit(solution)/shard_map/while/body/eval_jaxpr/hqk,khd->hqd/dot_general | solution.py:38
  194.5 5.5 %fusion.25 = f32[12,1024,64]{1,2,0:T(8,128)} fusion(f32[12,1024,64]{1,2,0:T(8,128)} %get-tuple-element.187, f32[12,1024]{1,0:T(8,128)S(1)} %get-tuple-element.173, pred[]{:T(512)S(6)} %compare.3, bf16[16,128,12,64]{1,3,2,0:T(8,128)(2,1)} %get-tuple-element.201, s32[]{:T(128)} %get-tuple-element.184, f32[12,128,1024]{2,1,0:T(8,128)S(1)} %copy-done.1, ...), kind=kOutput, calls=%fused_computation.7.clone.1 | convolution fusion | flops 209977344 | bytes 12878465 | tf_op jit(solution)/shard_map/while/body/eval_jaxpr/hqk,khd->hqd/dot_general | solution.py:38
  209.5 5.5 %fusion.25 = f32[12,1024,64]{1,2,0:T(8,128)} fusion(f32[12,1024,64]{1,2,0:T(8,128)} %get-tuple-element.187, f32[12,1024]{1,0:T(8,128)S(1)} %get-tuple-element.173, pred[]{:T(512)S(6)} %compare.3, bf16[16,128,12,64]{1,3,2,0:T(8,128)(2,1)} %get-tuple-element.201, s32[]{:T(128)} %get-tuple-element.184, f32[12,128,1024]{2,1,0:T(8,128)S(1)} %copy-done.1, ...), kind=kOutput, calls=%fused_computation.7.clone.1 | convolution fusion | flops 209977344 | bytes 12878465 | tf_op jit(solution)/shard_map/while/body/eval_jaxpr/hqk,khd->hqd/dot_general | solution.py:38
  224.5 5.5 %fusion.25 = f32[12,1024,64]{1,2,0:T(8,128)} fusion(f32[12,1024,64]{1,2,0:T(8,128)} %get-tuple-element.187, f32[12,1024]{1,0:T(8,128)S(1)} %get-tuple-element.173, pred[]{:T(512)S(6)} %compare.3, bf16[16,128,12,64]{1,3,2,0:T(8,128)(2,1)} %get-tuple-element.201, s32[]{:T(128)} %get-tuple-element.184, f32[12,128,1024]{2,1,0:T(8,128)S(1)} %copy-done.1, ...), kind=kOutput, calls=%fused_computation.7.clone.1 | convolution fusion | flops 209977344 | bytes 12878465 | tf_op jit(solution)/shard_map/while/body/eval_jaxpr/hqk,khd->hqd/dot_general | solution.py:38
  239.5 5.5 %fusion.25 = f32[12,1024,64]{1,2,0:T(8,128)} fusion(f32[12,1024,64]{1,2,0:T(8,128)} %get-tuple-element.187, f32[12,1024]{1,0:T(8,128)S(1)} %get-tuple-element.173, pred[]{:T(512)S(6)} %compare.3, bf16[16,128,12,64]{1,3,2,0:T(8,128)(2,1)} %get-tuple-element.201, s32[]{:T(128)} %get-tuple-element.184, f32[12,128,1024]{2,1,0:T(8,128)S(1)} %copy-done.1, ...), kind=kOutput, calls=%fused_computation.7.clone.1 | convolution fusion | flops 209977344 | bytes 12878465 | tf_op jit(solution)/shard_map/while/body/eval_jaxpr/hqk,khd->hqd/dot_general | solution.py:38
  254.5 5.5 %fusion.25 = f32[12,1024,64]{1,2,0:T(8,128)} fusion(f32[12,1024,64]{1,2,0:T(8,128)} %get-tuple-element.187, f32[12,1024]{1,0:T(8,128)S(1)} %get-tuple-element.173, pred[]{:T(512)S(6)} %compare.3, bf16[16,128,12,64]{1,3,2,0:T(8,128)(2,1)} %get-tuple-element.201, s32[]{:T(128)} %get-tuple-element.184, f32[12,128,1024]{2,1,0:T(8,128)S(1)} %copy-done.1, ...), kind=kOutput, calls=%fused_computation.7.clone.1 | convolution fusion | flops 209977344 | bytes 12878465 | tf_op jit(solution)/shard_map/while/body/eval_jaxpr/hqk,khd->hqd/dot_general | solution.py:38
  269.4 5.5 %fusion.25 = f32[12,1024,64]{1,2,0:T(8,128)} fusion(f32[12,1024,64]{1,2,0:T(8,128)} %get-tuple-element.187, f32[12,1024]{1,0:T(8,128)S(1)} %get-tuple-element.173, pred[]{:T(512)S(6)} %compare.3, bf16[16,128,12,64]{1,3,2,0:T(8,128)(2,1)} %get-tuple-element.201, s32[]{:T(128)} %get-tuple-element.184, f32[12,128,1024]{2,1,0:T(8,128)S(1)} %copy-done.1, ...), kind=kOutput, calls=%fused_computation.7.clone.1 | convolution fusion | flops 209977344 | bytes 12878465 | tf_op jit(solution)/shard_map/while/body/eval_jaxpr/hqk,khd->hqd/dot_general | solution.py:38
  284.4 5.5 %fusion.25 = f32[12,1024,64]{1,2,0:T(8,128)} fusion(f32[12,1024,64]{1,2,0:T(8,128)} %get-tuple-element.187, f32[12,1024]{1,0:T(8,128)S(1)} %get-tuple-element.173, pred[]{:T(512)S(6)} %compare.3, bf16[16,128,12,64]{1,3,2,0:T(8,128)(2,1)} %get-tuple-element.201, s32[]{:T(128)} %get-tuple-element.184, f32[12,128,1024]{2,1,0:T(8,128)S(1)} %copy-done.1, ...), kind=kOutput, calls=%fused_computation.7.clone.1 | convolution fusion | flops 209977344 | bytes 12878465 | tf_op jit(solution)/shard_map/while/body/eval_jaxpr/hqk,khd->hqd/dot_general | solution.py:38
  299.4 5.5 %fusion.25 = f32[12,1024,64]{1,2,0:T(8,128)} fusion(f32[12,1024,64]{1,2,0:T(8,128)} %get-tuple-element.187, f32[12,1024]{1,0:T(8,128)S(1)} %get-tuple-element.173, pred[]{:T(512)S(6)} %compare.3, bf16[16,128,12,64]{1,3,2,0:T(8,128)(2,1)} %get-tuple-element.201, s32[]{:T(128)} %get-tuple-element.184, f32[12,128,1024]{2,1,0:T(8,128)S(1)} %copy-done.1, ...), kind=kOutput, calls=%fused_computation.7.clone.1 | convolution fusion | flops 209977344 | bytes 12878465 | tf_op jit(solution)/shard_map/while/body/eval_jaxpr/hqk,khd->hqd/dot_general | solution.py:38
  314.4 5.5 %fusion.25 = f32[12,1024,64]{1,2,0:T(8,128)} fusion(f32[12,1024,64]{1,2,0:T(8,128)} %get-tuple-element.187, f32[12,1024]{1,0:T(8,128)S(1)} %get-tuple-element.173, pred[]{:T(512)S(6)} %compare.3, bf16[16,128,12,64]{1,3,2,0:T(8,128)(2,1)} %get-tuple-element.201, s32[]{:T(128)} %get-tuple-element.184, f32[12,128,1024]{2,1,0:T(8,128)S(1)} %copy-done.1, ...), kind=kOutput, calls=%fused_computation.7.clone.1 | convolution fusion | flops 209977344 | bytes 12878465 | tf_op jit(solution)/shard_map/while/body/eval_jaxpr/hqk,khd->hqd/dot_general | solution.py:38
  329.4 5.5 %fusion.25 = f32[12,1024,64]{1,2,0:T(8,128)} fusion(f32[12,1024,64]{1,2,0:T(8,128)} %get-tuple-element.187, f32[12,1024]{1,0:T(8,128)S(1)} %get-tuple-element.173, pred[]{:T(512)S(6)} %compare.3, bf16[16,128,12,64]{1,3,2,0:T(8,128)(2,1)} %get-tuple-element.201, s32[]{:T(128)} %get-tuple-element.184, f32[12,128,1024]{2,1,0:T(8,128)S(1)} %copy-done.1, ...), kind=kOutput, calls=%fused_computation.7.clone.1 | convolution fusion | flops 209977344 | bytes 12878465 | tf_op jit(solution)/shard_map/while/body/eval_jaxpr/hqk,khd->hqd/dot_general | solution.py:38
  344.3 5.5 %fusion.25 = f32[12,1024,64]{1,2,0:T(8,128)} fusion(f32[12,1024,64]{1,2,0:T(8,128)} %get-tuple-element.187, f32[12,1024]{1,0:T(8,128)S(1)} %get-tuple-element.173, pred[]{:T(512)S(6)} %compare.3, bf16[16,128,12,64]{1,3,2,0:T(8,128)(2,1)} %get-tuple-element.201, s32[]{:T(128)} %get-tuple-element.184, f32[12,128,1024]{2,1,0:T(8,128)S(1)} %copy-done.1, ...), kind=kOutput, calls=%fused_computation.7.clone.1 | convolution fusion | flops 209977344 | bytes 12878465 | tf_op jit(solution)/shard_map/while/body/eval_jaxpr/hqk,khd->hqd/dot_general | solution.py:38
  359.3 5.5 %fusion.25 = f32[12,1024,64]{1,2,0:T(8,128)} fusion(f32[12,1024,64]{1,2,0:T(8,128)} %get-tuple-element.187, f32[12,1024]{1,0:T(8,128)S(1)} %get-tuple-element.173, pred[]{:T(512)S(6)} %compare.3, bf16[16,128,12,64]{1,3,2,0:T(8,128)(2,1)} %get-tuple-element.201, s32[]{:T(128)} %get-tuple-element.184, f32[12,128,1024]{2,1,0:T(8,128)S(1)} %copy-done.1, ...), kind=kOutput, calls=%fused_computation.7.clone.1 | convolution fusion | flops 209977344 | bytes 12878465 | tf_op jit(solution)/shard_map/while/body/eval_jaxpr/hqk,khd->hqd/dot_general | solution.py:38
  364.9 33.8 %pmax.7 = f32[12,1024]{1,0:T(8,128)S(1)} all-reduce(f32[12,1024]{1,0:T(8,128)S(1)} %get-tuple-element.50), channel_id=1, replica_groups=mesh['blk'=8,'inner'=16] {'blk'}, use_global_device_ids=true, to_apply=%region_4.5 | all-reduce | flops 12288 | bytes 98304 | tf_op jit(solution)/shard_map/pmax | solution.py:60
  403.5 29.9 %reduce-scatter.5.cloned.1.call-done = f32[12,128]{1,0:T(8,128)} async-done(((f32[12,1024]{1,0:T(8,128)}), f32[12,128]{1,0:T(8,128)}) %reduce-scatter.5.cloned.1.call-update) | async-done | bytes 6160 | tf_op jit(solution)/shard_map/reduce_scatter | solution.py:63
  434.1 46.5 %reduce-scatter.3.cloned.1.call-done = f32[12,128,64]{1,2,0:T(8,128)} async-done(((f32[12,1024,64]{1,2,0:T(8,128)}), f32[12,128,64]{1,2,0:T(8,128)}) %reduce-scatter.3.cloned.1.call-update) | async-done | bytes 393232 | tf_op jit(solution)/shard_map/reduce_scatter | solution.py:64
  (157 shorter events, 170.0 us)
Async XLA Ops:
  6.5 475.1 %copy-start = (bf16[768,768]{1,0:T(8,128)(2,1)S(1)}, bf16[768,768]{1,0:T(8,128)(2,1)}, u32[]{:S(2)}) copy-start(bf16[768,768]{1,0:T(8,128)(2,1)} %param.11) | copy-start | bytes 3538948
  6.5 80.4 %all-gather.4.cloned.1.call-start = ((), (), s32[]{:S(2)}) async-start(), calls=%async_computation.3 | async-start | bytes 1769472 | tf_op jit(solution)/shard_map/all_gather | solution.py:74
  7.3 108.9 %all-gather.6.cloned.1.call-start = ((), (), s32[]{:S(2)}) async-start(), calls=%async_computation.4 | async-start | bytes 3342336 | tf_op jit(solution)/shard_map/all_gather | solution.py:82
  11.4 8.1 %copy-start.2 = (s32[128]{0:T(128)S(1)}, s32[128]{0:T(128)}, u32[]{:S(2)}) copy-start(s32[128]{0:T(128)} %param.10) | copy-start | bytes 1540
  11.4 114.9 %all-to-all-start = ((bf16[16,128,768]{1,2,0:T(8,128)(2,1)}), bf16[16,128,768]{1,2,0:T(8,128)(2,1)}, u32[]{:S(2)}, u32[]{:S(2)}) async-start(bf16[16,128,768]{1,2,0:T(8,128)(2,1)} %stack.2), calls=%async_computation | async-start | bytes 6291456 | tf_op jit(solution)/shard_map/all_to_all | solution.py:80
  19.3 414.0 %reduce-scatter.5.cloned.1.call-start = ((), (), s32[]{:S(2)}) async-start(), calls=%async_computation.6 | async-start | bytes 73728 | tf_op jit(solution)/shard_map/reduce_scatter | solution.py:63
  131.1 4.6 copy-start.1
  145.0 4.6 copy-start.1
  160.0 4.6 copy-start.1
  175.0 4.6 copy-start.1
  189.9 4.6 copy-start.1
  204.9 4.6 copy-start.1
  219.9 4.6 copy-start.1
  234.9 4.6 copy-start.1
  249.9 4.6 copy-start.1
  264.8 4.6 copy-start.1
  279.8 4.6 copy-start.1
  294.8 4.6 copy-start.1
  309.8 4.6 copy-start.1
  324.8 4.6 copy-start.1
  339.7 4.6 copy-start.1
  354.7 4.6 copy-start.1
  399.3 81.3 %reduce-scatter.3.cloned.1.call-start = ((), (), s32[]{:S(2)}) async-start(), calls=%async_computation.5 | async-start | bytes 3538944 | tf_op jit(solution)/shard_map/reduce_scatter | solution.py:64
Sparse Core Ops, SparseCore 0:
  9.0 50.5 all-gather.3
  62.0 54.0 all-gather.5
  399.4 33.9 reduce-scatter.4
  435.8 44.7 reduce-scatter.2
